TPU v7x, 32 devices: a whole 2x2x4 slice. The times are simulated.
32 devices in a mesh: obs: 4 (over z), src: 8 (over y, x, core).
Axes of the slice: x: 2, y: 2, z: 4, core: 2. Of those that a mesh axis runs over, the one named last changes fastest.
Arguments:
- history: bfloat16 [3, 64, 64, 1536], P(None, ('obs', 'src')), may hold values from -6 to 6
- incident: bfloat16 [5, 64, 64, 1536], P(None, ('obs', 'src')), may hold values from -6 to 6
- proj_basis: bfloat16 [64, 64, 1536], P(('obs', 'src')), may hold values from -0.15625 to 0.15625
- expand_basis: bfloat16 [64, 64, 1536], P(('obs', 'src')), may hold values from -0.75 to 0.75
- near_inverse: bfloat16 [64, 1536, 1536], P(('obs', 'src')), may hold values from -0.15625 to 0.15625
- couplings: bfloat16 [2, 4096, 4, 8, 128], P(None, 'obs', None, 'src'), may hold values from -0.09375 to 0.09375
- lags: int32 [64, 4, 8, 2], P('obs', None, 'src'), may hold values from 0 to 2, as said below
Outputs:
- currents: bfloat16 [5, 64, 64, 1536], P(None, ('obs', 'src'))
Inputs may be any that keep to these rules, and one draw needn't show every extreme that they name: lags[j, o, s, k] is the lag from source cluster j to observer cluster (o * 8 + s) * 2 + k. Entries are 0, 1 or 2, and the entry of every cluster with itself is 0.
All inputs are finite; a program needn't handle non-finite values.
Results may differ from a plain program's by a relative error of at most 0.025.
Values may be sent and summed in bfloat16 or wider, within the bound.
A program may use at most 192 MiB of HBM per device.

v0:
```python
import jax
import jax.numpy as jnp
from jax import lax
from jax.sharding import PartitionSpec as P

STEPS = 5
TAPS = 2
HIST = 3


def per_device(history, incident, proj_basis, expand_basis, near_inverse, couplings, lags):
    rank = proj_basis.shape[1]
    local_clusters = proj_basis.shape[0]
    excite = history.shape[2]
    src_rows = couplings.shape[1]
    obs_cols = couplings.shape[2] * couplings.shape[3] * couplings.shape[4]
    src_clusters = lags.shape[0]
    obs_clusters = lags.shape[1] * lags.shape[2] * lags.shape[3]
    kernel = couplings.reshape(TAPS, src_clusters, rank, obs_clusters, rank)
    lag_pairs = lags.reshape(src_clusters, obs_clusters)
    matrices = []
    for delay in range(1, HIST + 1):
        combined = jnp.zeros_like(kernel[0])
        for tap_index in range(TAPS):
            if delay - tap_index >= 1:
                chosen = (lag_pairs == delay - tap_index)[:, None, :, None]
                combined = jnp.where(chosen, kernel[tap_index], combined)
        matrices.append(combined.reshape(src_rows, obs_cols))

    def project(current):
        projected = jnp.einsum(
            "ceb,crb->ecr", current, proj_basis, preferred_element_type=jnp.float32
        )
        return projected.astype(jnp.bfloat16).reshape(excite, local_clusters * rank)

    def couple(columns, delay):
        return jnp.dot(columns, matrices[delay - 1], preferred_element_type=jnp.float32)

    stacked = jnp.stack([project(history[slot_index]) for slot_index in range(HIST)])
    gathered = lax.all_gather(stacked, "src", axis=2, tiled=True)
    past = [gathered[slot_index] for slot_index in range(HIST)]
    results = []
    latest = None
    for step in range(STEPS):
        if step > 0:
            newest = lax.all_gather(latest, "src", axis=1, tiled=True)
            past = past[1:] + [newest]
        partial_value = couple(past[-1], 1) + couple(past[-2], 2) + couple(past[-3], 3)
        field = lax.psum_scatter(
            partial_value.astype(jnp.bfloat16), "obs", scatter_dimension=1, tiled=True
        )
        field_cast = field.reshape(excite, local_clusters, rank)
        far_field = jnp.einsum(
            "ecr,crb->ceb", field_cast, expand_basis, preferred_element_type=jnp.float32
        )
        residual_field = (incident[step].astype(jnp.float32) - far_field).astype(jnp.bfloat16)
        current = jnp.einsum(
            "ceb,cbd->ced", residual_field, near_inverse, preferred_element_type=jnp.float32
        ).astype(jnp.bfloat16)
        results.append(current)
        if step + 1 < STEPS:
            latest = project(current)
    return jnp.stack(results)


def solution(mesh):
    placed = (
        P(None, ("obs", "src"), None, None),
        P(None, ("obs", "src"), None, None),
        P(("obs", "src"), None, None),
        P(("obs", "src"), None, None),
        P(("obs", "src"), None, None),
        P(None, "obs", None, "src", None),
        P("obs", None, "src", None),
    )
    return jax.shard_map(
        per_device,
        mesh=mesh,
        in_specs=placed,
        out_specs=P(None, ("obs", "src"), None, None),
        check_vma=False,
    )
```

profile of v0, /device:TPU:0, one launch (start us, length us, event | category | flops | bytes accessed | tf_op | source)
XLA Modules:
  0.0 237.1 jit_solution(1757093044412803134)
XLA Ops:
  11.1 2.3 fusion.46
  13.3 2.0 squeeze.40
  15.3 1.8 squeeze.42
  17.2 4.3 %select_select_fusion = (bf16[16,64,8,64]{3,2,1,0:T(8,128)(2,1)}, bf16[16,64,8,64]{3,2,1,0:T(8,128)(2,1)}, bf16[16,64,8,64]{3,2,1,0:T(8,128)(2,1)}) fusion(bf16[16,64,8,64]{3,2,1,0:T(8,128)(2,1)} %squeeze.42, bf16[16,64,8,64]{3,2,1,0:T(8,128)(2,1)} %squeeze.40, pred[16,8]{1,0:T(8,128)(4,1)S(1)} %copy.20, pred[16,8]{1,0:T(8,128)(4,1)S(1)} %copy.19, ...), kind=kLoop, calls=%fused_computation.17 | loop fusion | flops 2621440 | bytes 5243264 | tf_op jit(solution)/shard_map/jit(_where)/select_n | solution.py:27
  21.5 4.0 %select_n.97 = bf16[1024,512]{1,0:T(8,128)(2,1)} reshape(bf16[16,64,8,64]{3,2,1,0:T(8,128)(2,1)} %get-tuple-element.7) | data formatting | bytes 2097152 | tf_op jit(solution)/shard_map/jit(_where)/select_n | solution.py:27
  25.6 11.9 %all_gather.15 = bf16[3,64,1024]{1,2,0:T(8,128)(2,1)S(1)} all-gather(bf16[3,64,128]{1,2,0:T(8,128)(2,1)S(1)} %pad_maximum_fusion), channel_id=1, replica_groups=mesh['obs'=4,'src'=8] {'src'}, dimensions={2}, use_global_device_ids=true | all-gather | bytes 442368 | tf_op jit(solution)/shard_map/all_gather | solution.py:40
  37.5 3.5 %select_n.100 = bf16[1024,512]{1,0:T(8,128)(2,1)S(1)} reshape(bf16[16,64,8,64]{3,2,1,0:T(8,128)(2,1)} %get-tuple-element.6) | data formatting | bytes 2097152 | tf_op jit(solution)/shard_map/jit(_where)/select_n | solution.py:27
  41.0 3.2 %select_n.103 = bf16[1024,512]{1,0:T(8,128)(2,1)S(1)} reshape(bf16[16,64,8,64]{3,2,1,0:T(8,128)(2,1)} %get-tuple-element.5) | data formatting | bytes 2097152 | tf_op jit(solution)/shard_map/jit(_where)/select_n | solution.py:27
  48.5 2.7 %broadcast_in_dim.38 = pred[1024,512]{1,0:T(32,128)(4,1)} reshape(pred[16,64,8,64]{3,2,1,0:T(8,128)(4,1)S(1)} %broadcast_in_dim.35) | data formatting | bytes 1048576 | tf_op jit(solution)/shard_map/jit(_where)/broadcast_in_dim | solution.py:27
  51.6 2.7 %broadcast_in_dim.39 = pred[1024,512]{1,0:T(32,128)(4,1)} reshape(pred[16,64,8,64]{3,2,1,0:T(8,128)(4,1)S(1)} %broadcast_in_dim.36) | data formatting | bytes 1048576 | tf_op jit(solution)/shard_map/jit(_where)/broadcast_in_dim | solution.py:27
  54.3 2.5 %bitcast_select_fusion.1 = bf16[1024,512]{1,0:T(8,128)(2,1)S(1)} fusion(pred[1024,512]{1,0:T(32,128)(4,1)} %broadcast_in_dim.38, pred[1024,512]{1,0:T(32,128)(4,1)} %broadcast_in_dim.39, bf16[128,8,4,128]{3,2,1,0:T(4,128)(2,1)} %bitcast.199, bf16[128,8,4,128]{3,2,1,0:T(4,128)(2,1)} %bitcast.202), kind=kLoop, calls=%fused_computation.47 | loop fusion | flops 1048576 | bytes 4194304 | tf_op jit(solution)/shard_map/jit(_where)/select_n | solution.py:27
  56.8 1.9 fusion.41
  58.8 8.2 %reduce-scatter.16.cloned.1.call-done = bf16[128,64]{1,0:T(8,128)(2,1)} async-done(((bf16[512,64]{1,0:T(8,128)(2,1)}), bf16[128,64]{1,0:T(8,128)(2,1)}) %reduce-scatter.16.cloned.1.call-update) | async-done | bytes 16400
  67.0 6.7 %bitcast_dynamic-update-slice_fusion.3 = (bf16[5,2,64,1536]{3,2,1,0:T(8,128)(2,1)}, bf16[2,64,1536]{2,1,0:T(8,128)(2,1)}) fusion(bf16[2,1536,1536]{2,1,0:T(8,128)(2,1)} %param.11, bf16[64,2,64]{0,2,1:T(8,128)(2,1)} %bitcast.214, bf16[2,64,1536]{2,1,0:T(8,128)(2,1)S(1)} %copy-done, bf16[5,2,64,1536]{3,2,1,0:T(8,128)(2,1)} %param.8), kind=kOutput, calls=%fused_computation.64 | convolution fusion | flops 629932032 | bytes 11042816 | tf_op jit(solution)/shard_map/ceb,cbd->ced/dot_general | solution.py:57
  76.6 9.2 %all_gather.16 = bf16[64,1024]{1,0:T(8,128)(2,1)S(1)} all-gather(bf16[64,128]{1,0:T(8,128)(2,1)S(1)} %reshape.176), channel_id=1, replica_groups=mesh['obs'=4,'src'=8] {'src'}, dimensions={1}, use_global_device_ids=true | all-gather | bytes 147456 | tf_op jit(solution)/shard_map/all_gather | solution.py:46
  86.5 2.3 fusion.13
  88.7 1.6 copy.32
  90.4 1.9 fusion.40
  92.3 14.9 %reduce-scatter.18.cloned.1.call-done = bf16[128,64]{1,0:T(8,128)(2,1)} async-done(((bf16[512,64]{1,0:T(8,128)(2,1)}), bf16[128,64]{1,0:T(8,128)(2,1)}) %reduce-scatter.18.cloned.1.call-update) | async-done | bytes 16400
  107.2 6.7 %bitcast_dynamic-update-slice_fusion.2 = (bf16[5,2,64,1536]{3,2,1,0:T(8,128)(2,1)}, bf16[2,64,1536]{2,1,0:T(8,128)(2,1)}) fusion(bf16[5,2,64,1536]{3,2,1,0:T(8,128)(2,1)} %get-tuple-element.13, bf16[2,1536,1536]{2,1,0:T(8,128)(2,1)} %param.11, bf16[64,2,64]{0,2,1:T(8,128)(2,1)} %bitcast.216, bf16[2,64,1536]{2,1,0:T(8,128)(2,1)S(1)} %copy-done, ...), kind=kOutput, calls=%fused_computation.63 | convolution fusion | flops 629932032 | bytes 11042816 | tf_op jit(solution)/shard_map/ceb,cbd->ced/dot_general | solution.py:57
  116.7 9.1 %all_gather.17 = bf16[64,1024]{1,0:T(8,128)(2,1)S(1)} all-gather(bf16[64,128]{1,0:T(8,128)(2,1)S(1)} %reshape.178), channel_id=1, replica_groups=mesh['obs'=4,'src'=8] {'src'}, dimensions={1}, use_global_device_ids=true | all-gather | bytes 147456 | tf_op jit(solution)/shard_map/all_gather | solution.py:46
  129.0 4.0 %broadcast_in_dim.40 = pred[1024,512]{1,0:T(32,128)(4,1)} reshape(pred[16,64,8,64]{3,2,1,0:T(8,128)(4,1)} %broadcast_in_dim.37) | data formatting | bytes 1048576 | tf_op jit(solution)/shard_map/jit(_where)/broadcast_in_dim | solution.py:27
  133.0 11.5 %reduce-scatter.20.cloned.1.call-done = bf16[128,64]{1,0:T(8,128)(2,1)} async-done(((bf16[512,64]{1,0:T(8,128)(2,1)}), bf16[128,64]{1,0:T(8,128)(2,1)}) %reduce-scatter.20.cloned.1.call-update) | async-done | bytes 16400
  144.5 6.6 %bitcast_dynamic-update-slice_fusion.1 = (bf16[5,2,64,1536]{3,2,1,0:T(8,128)(2,1)}, bf16[2,64,1536]{2,1,0:T(8,128)(2,1)S(1)}) fusion(bf16[5,2,64,1536]{3,2,1,0:T(8,128)(2,1)} %get-tuple-element.15, bf16[2,1536,1536]{2,1,0:T(8,128)(2,1)} %param.11, bf16[64,2,64]{0,2,1:T(8,128)(2,1)} %bitcast.215, bf16[2,64,1536]{2,1,0:T(8,128)(2,1)S(1)} %copy-done, ...), kind=kOutput, calls=%fused_computation.62 | convolution fusion | flops 629932032 | bytes 11042816 | tf_op jit(solution)/shard_map/ceb,cbd->ced/dot_general | solution.py:57
  152.9 9.1 %all_gather.18 = bf16[64,1024]{1,0:T(8,128)(2,1)S(1)} all-gather(bf16[64,128]{1,0:T(8,128)(2,1)S(1)} %reshape.180), channel_id=1, replica_groups=mesh['obs'=4,'src'=8] {'src'}, dimensions={1}, use_global_device_ids=true | all-gather | bytes 147456 | tf_op jit(solution)/shard_map/all_gather | solution.py:46
  162.7 1.6 fusion.44
  166.1 1.6 copy.36
  167.8 16.8 %reduce-scatter.22.cloned.1.call-done = bf16[128,64]{1,0:T(8,128)(2,1)} async-done(((bf16[512,64]{1,0:T(8,128)(2,1)}), bf16[128,64]{1,0:T(8,128)(2,1)}) %reduce-scatter.22.cloned.1.call-update) | async-done | bytes 16400
  184.6 6.7 %bitcast_dynamic-update-slice_fusion = (bf16[5,2,64,1536]{3,2,1,0:T(8,128)(2,1)}, bf16[2,64,1536]{2,1,0:T(8,128)(2,1)}) fusion(bf16[5,2,64,1536]{3,2,1,0:T(8,128)(2,1)} %get-tuple-element.17, bf16[2,1536,1536]{2,1,0:T(8,128)(2,1)} %param.11, bf16[64,2,64]{0,2,1:T(8,128)(2,1)} %bitcast.217, bf16[2,64,1536]{2,1,0:T(8,128)(2,1)S(1)} %copy-done, ...), kind=kOutput, calls=%fused_computation.61 | convolution fusion | flops 629932032 | bytes 11042816 | tf_op jit(solution)/shard_map/ceb,cbd->ced/dot_general | solution.py:57
  194.2 9.4 %all_gather.19 = bf16[64,1024]{1,0:T(8,128)(2,1)S(1)} all-gather(bf16[64,128]{1,0:T(8,128)(2,1)S(1)} %reshape.182), channel_id=1, replica_groups=mesh['obs'=4,'src'=8] {'src'}, dimensions={1}, use_global_device_ids=true | all-gather | bytes 147456 | tf_op jit(solution)/shard_map/all_gather | solution.py:46
  207.1 16.9 %reduce-scatter.24.cloned.1.call-done = bf16[128,64]{1,0:T(8,128)(2,1)} async-done(((bf16[512,64]{1,0:T(8,128)(2,1)}), bf16[128,64]{1,0:T(8,128)(2,1)}) %reduce-scatter.24.cloned.1.call-update) | async-done | bytes 16400
  224.0 6.6 %fusion.6 = bf16[5,2,64,1536]{3,2,1,0:T(8,128)(2,1)} fusion(bf16[5,2,64,1536]{3,2,1,0:T(8,128)(2,1)} %get-tuple-element.19, bf16[2,1536,1536]{2,1,0:T(8,128)(2,1)} %param.11, bf16[64,2,64]{0,2,1:T(8,128)(2,1)} %bitcast.218, bf16[2,64,1536]{2,1,0:T(8,128)(2,1)S(1)} %copy-done, bf16[5,2,64,1536]{3,2,1,0:T(8,128)(2,1)} %param.8), kind=kOutput, calls=%fused_computation.16 | convolution fusion | flops 629932032 | bytes 10649600 | tf_op jit(solution)/shard_map/ceb,cbd->ced/dot_general | solution.py:57
  (98 shorter events, 29.2 us)
Async XLA Ops:
  6.5 60.5 %copy-start = (bf16[2,64,1536]{2,1,0:T(8,128)(2,1)S(1)}, bf16[2,64,1536]{2,1,0:T(8,128)(2,1)}, u32[]{:S(2)}) copy-start(bf16[2,64,1536]{2,1,0:T(8,128)(2,1)} %param.10) | copy-start | bytes 1179652
  6.5 4.2 %copy-start.23 = (s32[16,4,1,2]{0,3,2,1:T(2,128)S(1)}, s32[16,4,1,2]{0,3,2,1:T(2,128)}, u32[]{:S(2)}) copy-start(s32[16,4,1,2]{0,3,2,1:T(2,128)} %param.13) | copy-start | bytes 1540
  6.5 60.5 %reduce-scatter.16.cloned.1.call-start = ((), (), s32[]{:S(2)}) async-start(), calls=%async_computation.5 | async-start | bytes 163840
  11.1 6.1 %copy-start.21 = (pred[16,8]{1,0:T(8,128)(4,1)}, pred[16,8]{1,0:T(8,128)(4,1)S(1)}, u32[]{:S(2)}) copy-start(pred[16,8]{1,0:T(8,128)(4,1)S(1)} %copy.20) | copy-start | bytes 388
  13.3 3.8 %copy-start.1 = (bf16[1,1024,4,1,128]{4,2,3,1,0:T(4,128)(2,1)}, bf16[1,1024,4,1,128]{4,2,3,1,0:T(4,128)(2,1)S(1)}, u32[]{:S(2)}) copy-start(bf16[1,1024,4,1,128]{4,2,3,1,0:T(4,128)(2,1)S(1)} %get-tuple-element.8) | copy-start | bytes 3145732
  13.3 3.8 %copy-start.3 = (bf16[1,1024,4,1,128]{4,2,3,1,0:T(4,128)(2,1)}, bf16[1,1024,4,1,128]{4,2,3,1,0:T(4,128)(2,1)S(1)}, u32[]{:S(2)}) copy-start(bf16[1,1024,4,1,128]{4,2,3,1,0:T(4,128)(2,1)S(1)} %get-tuple-element.9) | copy-start | bytes 3145732
  37.5 9.7 %copy-start.5 = (bf16[3,64,1024]{1,2,0:T(8,128)(2,1)}, bf16[3,64,1024]{1,2,0:T(8,128)(2,1)S(1)}, u32[]{:S(2)}) copy-start(bf16[3,64,1024]{1,2,0:T(8,128)(2,1)S(1)} %all_gather.15) | copy-start | bytes 1179652
  47.1 60.1 %reduce-scatter.18.cloned.1.call-start = ((), (), s32[]{:S(2)}) async-start(), calls=%async_computation.6 | async-start | bytes 163840
  67.0 19.4 %copy-start.4 = (bf16[1,1024,4,1,128]{4,2,3,1,0:T(4,128)(2,1)S(1)}, bf16[1,1024,4,1,128]{4,2,3,1,0:T(4,128)(2,1)}, u32[]{:S(2)}) copy-start(bf16[1,1024,4,1,128]{4,2,3,1,0:T(4,128)(2,1)} %copy-done.3) | copy-start | bytes 3145732
  85.8 0.6 copy-start.12
  90.4 54.2 %reduce-scatter.20.cloned.1.call-start = ((), (), s32[]{:S(2)}) async-start(), calls=%async_computation.7 | async-start | bytes 163840
  107.2 6.8 %copy-start.6 = (bf16[2,64,1536]{2,1,0:T(8,128)(2,1)S(1)}, bf16[2,64,1536]{2,1,0:T(8,128)(2,1)}, u32[]{:S(2)}) copy-start(bf16[2,64,1536]{2,1,0:T(8,128)(2,1)} %param.9) | copy-start | bytes 1179652
  107.2 18.7 %copy-start.9 = (pred[1024,512]{1,0:T(32,128)(4,1)S(1)}, pred[1024,512]{1,0:T(32,128)(4,1)}, u32[]{:S(2)}) copy-start(pred[1024,512]{1,0:T(32,128)(4,1)} %broadcast_in_dim.38) | copy-start | bytes 1572868
  114.0 12.6 %copy-start.13 = (bf16[64,1024]{1,0:T(8,128)(2,1)S(1)}, bf16[64,1024]{1,0:T(8,128)(2,1)}, u32[]{:S(2)}) copy-start(bf16[64,1024]{1,0:T(8,128)(2,1)} %copy-done.12) | copy-start | bytes 393220
  116.7 9.8 %copy-start.15 = (f32[64,512]{1,0:T(8,128)S(1)}, f32[64,512]{1,0:T(8,128)}, u32[]{:S(2)}) copy-start(f32[64,512]{1,0:T(8,128)} %fusion.40) | copy-start | bytes 393220
  125.9 0.7 copy-start.16
  125.9 1.8 copy-start.22
  127.6 57.0 %reduce-scatter.22.cloned.1.call-start = ((), (), s32[]{:S(2)}) async-start(), calls=%async_computation.8 | async-start | bytes 163840
  152.0 12.7 %copy-start.2 = (bf16[1,1024,4,1,128]{4,2,3,1,0:T(4,128)(2,1)S(1)}, bf16[1,1024,4,1,128]{4,2,3,1,0:T(4,128)(2,1)}, u32[]{:S(2)}) copy-start(bf16[1,1024,4,1,128]{4,2,3,1,0:T(4,128)(2,1)} %copy-done.1) | copy-start | bytes 3145732
  152.9 11.4 %copy-start.17 = (bf16[64,1024]{1,0:T(8,128)(2,1)S(1)}, bf16[64,1024]{1,0:T(8,128)(2,1)}, u32[]{:S(2)}) copy-start(bf16[64,1024]{1,0:T(8,128)(2,1)} %copy-done.16) | copy-start | bytes 393220
  152.9 11.7 %copy-start.7 = (pred[1024,512]{1,0:T(32,128)(4,1)S(1)}, pred[1024,512]{1,0:T(32,128)(4,1)}, u32[]{:S(2)}) copy-start(pred[1024,512]{1,0:T(32,128)(4,1)} %broadcast_in_dim.39) | copy-start | bytes 1572868
  152.9 11.7 %copy-start.10 = (pred[1024,512]{1,0:T(32,128)(4,1)S(1)}, pred[1024,512]{1,0:T(32,128)(4,1)}, u32[]{:S(2)}) copy-start(pred[1024,512]{1,0:T(32,128)(4,1)} %broadcast_in_dim.40) | copy-start | bytes 1572868
  152.9 11.7 %copy-start.14 = (bf16[64,1024]{1,0:T(8,128)(2,1)S(1)}, bf16[64,1024]{1,0:T(8,128)(2,1)}, u32[]{:S(2)}) copy-start(bf16[64,1024]{1,0:T(8,128)(2,1)} %copy-done.12) | copy-start | bytes 393220
  162.1 0.7 copy-start.19
  167.8 56.2 %reduce-scatter.24.cloned.1.call-start = ((), (), s32[]{:S(2)}) async-start(), calls=%async_computation.9 | async-start | bytes 163840
  194.1 11.0 %copy-start.20 = (bf16[64,1024]{1,0:T(8,128)(2,1)S(1)}, bf16[64,1024]{1,0:T(8,128)(2,1)}, u32[]{:S(2)}) copy-start(bf16[64,1024]{1,0:T(8,128)(2,1)} %copy-done.19) | copy-start | bytes 393220
  194.1 11.3 %copy-start.8 = (pred[1024,512]{1,0:T(32,128)(4,1)S(1)}, pred[1024,512]{1,0:T(32,128)(4,1)}, u32[]{:S(2)}) copy-start(pred[1024,512]{1,0:T(32,128)(4,1)} %broadcast_in_dim.39) | copy-start | bytes 1572868
  194.2 11.3 %copy-start.11 = (pred[1024,512]{1,0:T(32,128)(4,1)S(1)}, pred[1024,512]{1,0:T(32,128)(4,1)}, u32[]{:S(2)}) copy-start(pred[1024,512]{1,0:T(32,128)(4,1)} %broadcast_in_dim.40) | copy-start | bytes 1572868
  194.2 11.3 %copy-start.18 = (bf16[64,1024]{1,0:T(8,128)(2,1)S(1)}, bf16[64,1024]{1,0:T(8,128)(2,1)}, u32[]{:S(2)}) copy-start(bf16[64,1024]{1,0:T(8,128)(2,1)} %copy-done.16) | copy-start | bytes 393220
Sparse Core Ops, SparseCore 0:
  47.3 19.7 reduce-scatter.15
  90.5 16.6 reduce-scatter.17
  127.7 16.7 reduce-scatter.19
  167.9 16.6 reduce-scatter.21
  207.3 16.6 reduce-scatter.23
where the time goes:
time: 238 us; the launch traced here: 237 us
  waiting for transfers between devices  68.4 us (29%)
  matrix products  57.8 us (24%)
  blocking collectives  48.8 us (21%)
  local copies, waits for them, and re-layouts  41.5 us (17%)
  between operations  13.5 us (6%)
  other arithmetic  6.91 us (3%)
    unnamed x10, waiting for transfers between devices  68.4 us
    all_gather x4, blocking collectives, per_device(): newest = lax.all_gather(latest, 'src', axis=1, tiled=True)  36.9 us
    dot_general x5, matrix products, per_device(): jnp.einsum('ceb,cbd->ced', residual_field, near_inverse, preferred_elemen...  33.3 us
    dot_general x15, matrix products, couple(): jnp.dot(columns, matrices[delay - 1], preferred_element_type=jnp.float32)  16.1 us
    all_gather x1, blocking collectives, per_device(): gathered = lax.all_gather(stacked, 'src', axis=2, tiled=True)  11.9 us
    broadcast_in_dim x6, local copies, waits for them, and re-layouts, per_device(): combined = jnp.where(chosen, kernel[tap_index], combined)  11.4 us
    select_n x3, local copies, waits for them, and re-layouts, per_device(): combined = jnp.where(chosen, kernel[tap_index], combined)  10.7 us
    dot_general x7, matrix products, project(): jnp.einsum('ceb,crb->ecr', current, proj_basis, preferred_element_type=jn...  8.37 us
  transfers between devices with their start and end apart: 5, of which 5 were waited for; matrix products, arithmetic and copies ran while one was open for 8% of the time, Pallas kernels for 0%

commit v1 on v0

--- a/solution.py
+++ b/solution.py
@@ -43,7 +43,7 @@
     latest = None
     for step in range(STEPS):
         if step > 0:
-            newest = lax.all_gather(latest, "src", axis=1, tiled=True)
+            newest = jnp.concatenate(lax.all_gather(latest, "src"), axis=1)
             past = past[1:] + [newest]
         partial_value = couple(past[-1], 1) + couple(past[-2], 2) + couple(past[-3], 3)
         field = lax.psum_scatter(

time: 238 us -> 243 us (1.021)
  waiting for transfers between devices: 68.4 us -> 81.5 us
  local copies, waits for them, and re-layouts: 41.5 us -> 31.5 us
  matrix products: 57.8 us -> 61.4 us
  other arithmetic: 6.91 us -> 4.07 us
    unnamed x10, waiting for transfers between devices: 68.4 us -> 81.5 us
    broadcast_in_dim x6 -> x0, local copies, waits for them, and re-layouts: 11.4 us -> none  [per_device(): combined = jnp.where(chosen, kernel[tap_index], combined)]
    reshape x4 -> x0, local copies, waits for them, and re-layouts: 3.48 us -> none  [project(): return projected.astype(jnp.bfloat16).reshape(excite, local_clusters * rank)]
    another operation x0 -> x4, local copies, waits for them, and re-layouts: none -> 3.39 us  [per_device(): newest = jnp.concatenate(lax.all_gather(latest, 'src'), axis=1)]
    select_n x2 -> x1, other arithmetic: 6.87 us -> 4.03 us  [per_device(): combined = jnp.where(chosen, kernel[tap_index], combined)]
    unnamed x53 -> x21, local copies, waits for them, and re-layouts: 6.97 us -> 9.12 us
  transfers between devices with their start and end apart: 5 -> 5, of which waited for: 5 -> 5; matrix products, arithmetic and copies ran while one was open for 8% -> 2% of each run, Pallas kernels for 0% -> 0%
where the time goes in v1:
time: 243 us; the launch traced here: 242 us
  waiting for transfers between devices  81.5 us (34%)
  matrix products  61.4 us (25%)
  blocking collectives  50.1 us (21%)
  local copies, waits for them, and re-layouts  31.5 us (13%)
  between operations  13.4 us (6%)
  other arithmetic  4.07 us (2%)
    unnamed x10, waiting for transfers between devices  81.5 us
    all_gather x4, blocking collectives, per_device(): newest = jnp.concatenate(lax.all_gather(latest, 'src'), axis=1)  37.1 us
    dot_general x5, matrix products, per_device(): jnp.einsum('ceb,cbd->ced', residual_field, near_inverse, preferred_elemen...  33.3 us
    dot_general x15, matrix products, couple(): jnp.dot(columns, matrices[delay - 1], preferred_element_type=jnp.float32)  18.4 us
    all_gather x1, blocking collectives, per_device(): gathered = lax.all_gather(stacked, 'src', axis=2, tiled=True)  13 us
    dot_general x7, matrix products, project(): jnp.einsum('ceb,crb->ecr', current, proj_basis, preferred_element_type=jn...  9.65 us
    select_n x3, local copies, waits for them, and re-layouts, per_device(): combined = jnp.where(chosen, kernel[tap_index], combined)  9.58 us
    unnamed x21, local copies, waits for them, and re-layouts  9.12 us
  transfers between devices with their start and end apart: 5, of which 5 were waited for; matrix products, arithmetic and copies ran while one was open for 2% of the time, Pallas kernels for 0%

profile of v1, /device:TPU:0, one launch (start us, length us, event | category | flops | bytes accessed | tf_op | source)
XLA Modules:
  0.0 242.1 jit_solution(6981661725050741938)
XLA Ops:
  11.2 13.0 %all_gather.15 = bf16[3,64,1024]{1,2,0:T(8,128)(2,1)} all-gather(bf16[3,64,128]{1,2,0:T(8,128)(2,1)S(1)} %pad_maximum_fusion), channel_id=1, replica_groups=mesh['obs'=4,'src'=8] {'src'}, dimensions={2}, use_global_device_ids=true | all-gather | bytes 442368 | tf_op jit(solution)/shard_map/all_gather | solution.py:40
  24.1 1.7 fusion.64
  25.8 3.0 %squeeze.38 = bf16[16,64,8,64]{3,2,1,0:T(8,128)(2,1)S(1)} reshape(bf16[1,1024,4,1,128]{4,2,3,1,0:T(4,128)(2,1)} %get-tuple-element.8) | data formatting | bytes 2097152 | tf_op jit(solution)/shard_map/squeeze | solution.py:27
  28.9 1.9 squeeze.36
  30.7 4.0 %select_select_fusion = (bf16[16,64,8,64]{3,2,1,0:T(8,128)(2,1)}, bf16[16,64,8,64]{3,2,1,0:T(8,128)(2,1)}, bf16[16,64,8,64]{3,2,1,0:T(8,128)(2,1)}) fusion(bf16[16,64,8,64]{3,2,1,0:T(8,128)(2,1)S(1)} %squeeze.38, bf16[16,64,8,64]{3,2,1,0:T(8,128)(2,1)} %squeeze.36, pred[16,8]{1,0:T(8,128)(4,1)S(1)} %copy.24, pred[16,8]{1,0:T(8,128)(4,1)S(1)} %copy.23, ...), kind=kLoop, calls=%fused_computation.17 | loop fusion | flops 2621440 | bytes 5243264 | tf_op jit(solution)/shard_map/jit(_where)/select_n | solution.py:27
  34.8 3.2 %select_n.149 = bf16[1024,512]{1,0:T(8,128)(2,1)S(1)} reshape(bf16[16,64,8,64]{3,2,1,0:T(8,128)(2,1)} %get-tuple-element.5) | data formatting | bytes 2097152 | tf_op jit(solution)/shard_map/jit(_where)/select_n | solution.py:27
  38.0 3.2 %select_n.146 = bf16[1024,512]{1,0:T(8,128)(2,1)S(1)} reshape(bf16[16,64,8,64]{3,2,1,0:T(8,128)(2,1)} %get-tuple-element.6) | data formatting | bytes 2097152 | tf_op jit(solution)/shard_map/jit(_where)/select_n | solution.py:27
  41.2 3.2 %select_n.143 = bf16[1024,512]{1,0:T(8,128)(2,1)S(1)} reshape(bf16[16,64,8,64]{3,2,1,0:T(8,128)(2,1)} %get-tuple-element.7) | data formatting | bytes 2097152 | tf_op jit(solution)/shard_map/jit(_where)/select_n | solution.py:27
  46.9 1.9 fusion.11
  48.8 1.6 copy.38
  50.5 1.9 fusion.39
  52.4 1.9 fusion.41
  54.3 16.0 %reduce-scatter.16.cloned.1.call-done = bf16[128,64]{1,0:T(8,128)(2,1)} async-done(((bf16[512,64]{1,0:T(8,128)(2,1)}), bf16[128,64]{1,0:T(8,128)(2,1)}) %reduce-scatter.16.cloned.1.call-update) | async-done | bytes 16400
  70.3 6.7 %bitcast_dynamic-update-slice_fusion.3 = (bf16[5,2,64,1536]{3,2,1,0:T(8,128)(2,1)}, bf16[2,64,1536]{2,1,0:T(8,128)(2,1)}) fusion(bf16[2,1536,1536]{2,1,0:T(8,128)(2,1)} %param.11, bf16[64,2,64]{0,2,1:T(8,128)(2,1)} %bitcast.228, bf16[2,64,1536]{2,1,0:T(8,128)(2,1)S(1)} %copy-done, bf16[5,2,64,1536]{3,2,1,0:T(8,128)(2,1)} %param.8), kind=kOutput, calls=%fused_computation.59 | convolution fusion | flops 629932032 | bytes 11042816 | tf_op jit(solution)/shard_map/ceb,cbd->ced/dot_general | solution.py:57
  79.8 9.2 %all_gather.16 = bf16[8,64,128]{2,1,0:T(8,128)(2,1)S(1)} all-gather(bf16[1,64,128]{2,1,0:T(8,128)(2,1)S(1)} %all_gather_reshape.12), channel_id=1, replica_groups=mesh['obs'=4,'src'=8] {'src'}, dimensions={0}, use_global_device_ids=true | all-gather | bytes 147456 | tf_op jit(solution)/shard_map/all_gather | solution.py:46
  89.6 1.9 fusion.13
  91.5 1.6 copy.40
  93.2 1.9 fusion.40
  95.1 14.9 %reduce-scatter.18.cloned.1.call-done = bf16[128,64]{1,0:T(8,128)(2,1)} async-done(((bf16[512,64]{1,0:T(8,128)(2,1)}), bf16[128,64]{1,0:T(8,128)(2,1)}) %reduce-scatter.18.cloned.1.call-update) | async-done | bytes 16400
  110.0 6.7 %bitcast_dynamic-update-slice_fusion.2 = (bf16[5,2,64,1536]{3,2,1,0:T(8,128)(2,1)}, bf16[2,64,1536]{2,1,0:T(8,128)(2,1)}) fusion(bf16[5,2,64,1536]{3,2,1,0:T(8,128)(2,1)} %get-tuple-element.13, bf16[2,1536,1536]{2,1,0:T(8,128)(2,1)} %param.11, bf16[64,2,64]{0,2,1:T(8,128)(2,1)} %bitcast.227, bf16[2,64,1536]{2,1,0:T(8,128)(2,1)S(1)} %copy-done, ...), kind=kOutput, calls=%fused_computation.58 | convolution fusion | flops 629932032 | bytes 11042816 | tf_op jit(solution)/shard_map/ceb,cbd->ced/dot_general | solution.py:57
  119.5 9.3 %all_gather.17 = bf16[8,64,128]{2,1,0:T(8,128)(2,1)S(1)} all-gather(bf16[1,64,128]{2,1,0:T(8,128)(2,1)S(1)} %all_gather_reshape.13), channel_id=1, replica_groups=mesh['obs'=4,'src'=8] {'src'}, dimensions={0}, use_global_device_ids=true | all-gather | bytes 147456 | tf_op jit(solution)/shard_map/all_gather | solution.py:46
  129.8 1.9 fusion.12
  131.7 1.6 copy.42
  133.4 16.8 %reduce-scatter.20.cloned.1.call-done = bf16[128,64]{1,0:T(8,128)(2,1)} async-done(((bf16[512,64]{1,0:T(8,128)(2,1)}), bf16[128,64]{1,0:T(8,128)(2,1)}) %reduce-scatter.20.cloned.1.call-update) | async-done | bytes 16400
  150.2 6.7 %bitcast_dynamic-update-slice_fusion.1 = (bf16[5,2,64,1536]{3,2,1,0:T(8,128)(2,1)}, bf16[2,64,1536]{2,1,0:T(8,128)(2,1)}) fusion(bf16[5,2,64,1536]{3,2,1,0:T(8,128)(2,1)} %get-tuple-element.15, bf16[2,1536,1536]{2,1,0:T(8,128)(2,1)} %param.11, bf16[64,2,64]{0,2,1:T(8,128)(2,1)} %bitcast.229, bf16[2,64,1536]{2,1,0:T(8,128)(2,1)S(1)} %copy-done, ...), kind=kOutput, calls=%fused_computation.57 | convolution fusion | flops 629932032 | bytes 11042816 | tf_op jit(solution)/shard_map/ceb,cbd->ced/dot_general | solution.py:57
  159.8 9.3 %all_gather.18 = bf16[8,64,128]{2,1,0:T(8,128)(2,1)S(1)} all-gather(bf16[1,64,128]{2,1,0:T(8,128)(2,1)S(1)} %all_gather_reshape.14), channel_id=1, replica_groups=mesh['obs'=4,'src'=8] {'src'}, dimensions={0}, use_global_device_ids=true | all-gather | bytes 147456 | tf_op jit(solution)/shard_map/all_gather | solution.py:46
  172.2 1.6 copy.44
  173.9 16.8 %reduce-scatter.22.cloned.1.call-done = bf16[128,64]{1,0:T(8,128)(2,1)} async-done(((bf16[512,64]{1,0:T(8,128)(2,1)}), bf16[128,64]{1,0:T(8,128)(2,1)}) %reduce-scatter.22.cloned.1.call-update) | async-done | bytes 16400
  190.7 6.7 %bitcast_dynamic-update-slice_fusion = (bf16[5,2,64,1536]{3,2,1,0:T(8,128)(2,1)}, bf16[2,64,1536]{2,1,0:T(8,128)(2,1)}) fusion(bf16[5,2,64,1536]{3,2,1,0:T(8,128)(2,1)} %get-tuple-element.17, bf16[2,1536,1536]{2,1,0:T(8,128)(2,1)} %param.11, bf16[64,2,64]{0,2,1:T(8,128)(2,1)} %bitcast.230, bf16[2,64,1536]{2,1,0:T(8,128)(2,1)S(1)} %copy-done, ...), kind=kOutput, calls=%fused_computation.56 | convolution fusion | flops 629932032 | bytes 11042816 | tf_op jit(solution)/shard_map/ceb,cbd->ced/dot_general | solution.py:57
  200.2 9.3 %all_gather.19 = bf16[8,64,128]{2,1,0:T(8,128)(2,1)S(1)} all-gather(bf16[1,64,128]{2,1,0:T(8,128)(2,1)S(1)} %all_gather_reshape.15), channel_id=1, replica_groups=mesh['obs'=4,'src'=8] {'src'}, dimensions={0}, use_global_device_ids=true | all-gather | bytes 147456 | tf_op jit(solution)/shard_map/all_gather | solution.py:46
  212.1 16.9 %reduce-scatter.24.cloned.1.call-done = bf16[128,64]{1,0:T(8,128)(2,1)} async-done(((bf16[512,64]{1,0:T(8,128)(2,1)}), bf16[128,64]{1,0:T(8,128)(2,1)}) %reduce-scatter.24.cloned.1.call-update) | async-done | bytes 16400
  229.0 6.6 %fusion.6 = bf16[5,2,64,1536]{3,2,1,0:T(8,128)(2,1)} fusion(bf16[5,2,64,1536]{3,2,1,0:T(8,128)(2,1)} %get-tuple-element.19, bf16[2,1536,1536]{2,1,0:T(8,128)(2,1)} %param.11, bf16[64,2,64]{0,2,1:T(8,128)(2,1)} %bitcast.231, bf16[2,64,1536]{2,1,0:T(8,128)(2,1)S(1)} %copy-done, bf16[5,2,64,1536]{3,2,1,0:T(8,128)(2,1)} %param.8), kind=kOutput, calls=%fused_computation.16 | convolution fusion | flops 629932032 | bytes 10649600 | tf_op jit(solution)/shard_map/ceb,cbd->ced/dot_general | solution.py:57
  (59 shorter events, 25.9 us)
Async XLA Ops:
  6.5 63.7 %copy-start = (bf16[2,64,1536]{2,1,0:T(8,128)(2,1)S(1)}, bf16[2,64,1536]{2,1,0:T(8,128)(2,1)}, u32[]{:S(2)}) copy-start(bf16[2,64,1536]{2,1,0:T(8,128)(2,1)} %param.10) | copy-start | bytes 1179652
  6.5 4.3 %copy-start.7 = (s32[16,4,1,2]{0,3,2,1:T(2,128)S(1)}, s32[16,4,1,2]{0,3,2,1:T(2,128)}, u32[]{:S(2)}) copy-start(s32[16,4,1,2]{0,3,2,1:T(2,128)} %param.13) | copy-start | bytes 1540
  6.5 17.6 %copy-start.1 = (bf16[2,1024,4,1,128]{4,2,3,1,0:T(4,128)(2,1)S(1)}, bf16[2,1024,4,1,128]{4,2,3,1,0:T(4,128)(2,1)}, u32[]{:S(2)}) copy-start(bf16[2,1024,4,1,128]{4,2,3,1,0:T(4,128)(2,1)} %param.12) | copy-start | bytes 6291460
  6.5 63.7 %reduce-scatter.16.cloned.1.call-start = ((), (), s32[]{:S(2)}) async-start(), calls=%async_computation.5 | async-start | bytes 163840
  50.4 59.6 %reduce-scatter.18.cloned.1.call-start = ((), (), s32[]{:S(2)}) async-start(), calls=%async_computation.6 | async-start | bytes 163840
  89.0 0.6 copy-start.2
  93.1 57.1 %reduce-scatter.20.cloned.1.call-start = ((), (), s32[]{:S(2)}) async-start(), calls=%async_computation.7 | async-start | bytes 163840
  128.9 0.6 copy-start.4
  133.3 57.3 %reduce-scatter.22.cloned.1.call-start = ((), (), s32[]{:S(2)}) async-start(), calls=%async_computation.8 | async-start | bytes 163840
  159.8 11.5 %copy-start.3 = (bf16[8,64,128]{2,1,0:T(8,128)(2,1)S(1)}, bf16[8,64,128]{2,1,0:T(8,128)(2,1)}, u32[]{:S(2)}) copy-start(bf16[8,64,128]{2,1,0:T(8,128)(2,1)} %copy-done.2) | copy-start | bytes 393220
  169.1 0.7 copy-start.6
  173.8 55.2 %reduce-scatter.24.cloned.1.call-start = ((), (), s32[]{:S(2)}) async-start(), calls=%async_computation.9 | async-start | bytes 163840
  200.2 10.8 %copy-start.5 = (bf16[8,64,128]{2,1,0:T(8,128)(2,1)S(1)}, bf16[8,64,128]{2,1,0:T(8,128)(2,1)}, u32[]{:S(2)}) copy-start(bf16[8,64,128]{2,1,0:T(8,128)(2,1)} %copy-done.4) | copy-start | bytes 393220
Sparse Core Ops, SparseCore 0:
  50.5 19.6 reduce-scatter.15
  93.2 16.7 reduce-scatter.17
  133.5 16.7 reduce-scatter.19
  173.9 16.7 reduce-scatter.21
  212.3 16.6 reduce-scatter.23
